TPU v7x, 128 devices: a whole 4x4x4 slice. The times are simulated.
128 devices in a mesh: grp: 8 (over y_lo, z), tok: 16 (over y_hi, x, core).
Axes of the slice: x: 4, y: 4 (y_hi: 2, y_lo: 2; y = y_hi * 2 + y_lo), z: 4, core: 2. Of those that a mesh axis runs over, the one named last changes fastest.
Arguments:
- hidden: bfloat16 [8, 2048, 4608], P('grp', 'tok'), may hold values from -40 to 40
- input_gain: float32 [4608], replicated, may hold values from 0.25 to 1.75
- w_query: bfloat16 [4608, 4096], P(None, 'tok'), may hold values from -4 to 4
- w_key: bfloat16 [4608, 2048], P(None, 'tok'), may hold values from -4 to 4
- w_value: bfloat16 [4608, 2048], P(None, 'tok'), may hold values from -0.09375 to 0.09375
- w_out: bfloat16 [4096, 4608], P('tok'), may hold values from -0.09375 to 0.09375
- post_gain: float32 [4608], replicated, may hold values from 0.25 to 1.75
- cache_keys: bfloat16 [64, 256, 2048], P('grp', None, 'tok'), may hold values from -6 to 46
- cache_values: bfloat16 [64, 256, 2048], P('grp', None, 'tok'), may hold values from -6 to 6
- page_table: int32 [8, 8], replicated, may hold values from 0 to 63, as said below
- stretch_request: int32 [8, 8], P('grp'), may hold values from 0 to 2, never falling along the last dimension, each value on 1 to 4 neighbouring positions
- recompute_ids: int32 [8, 204], P('grp'), may hold values from 0 to 2047, as said below
- query_counts: int32 [8, 3], P('grp'), may hold values from 1 to 1024, 1844 in all within a row
Outputs:
- output: bfloat16 [8, 2048, 4608], P('grp', 'tok')
Inputs may be any that keep to these rules, and one draw needn't show every extreme that they name: `page_table`: row g lists the pages of group g's 8 stretch slots; page p is held by group p // 8; every page appears once, and the slots of a group take exactly one page from each group. `stretch_request`: each request of a group holds one or more consecutive slots, request numbers never fall along the slots, and one request holds (8 + 1) // 2 slots, none more. `recompute_ids`: each row holds 204 distinct cached tokens of the group (slot times 256 plus the token within the stretch) in rising order. `query_counts`: the counts of a group sum to 1844.
All inputs are finite; a program needn't handle non-finite values.
Results may differ from a plain program's by a relative error of at most 0.01.
Values may be sent and summed in bfloat16 or wider, within the bound.
A program may use at most 128 MiB of HBM per device.

v0:
```python
import math
import jax
import jax.numpy as jnp
from jax import lax
from jax.sharding import PartitionSpec as P

HEAD = 128
EPSILON = 1e-06
CAP_VALUE = 50.0
QUERY_SCALE = 1.0 / 12.0
ROPE_BASE = 10000.0


def rotate(tensor, positions):
    halfway = tensor.shape[-1] // 2
    ladder = jnp.arange(halfway).astype(jnp.float32)
    frequency = jnp.exp(ladder * (-2.0 * math.log(ROPE_BASE) / tensor.shape[-1]))
    angles = positions.astype(jnp.float32)[:, None] * frequency[None, :]
    cosine = jnp.cos(angles)[:, None, :]
    sine_values = jnp.sin(angles)[:, None, :]
    front_part = tensor[..., :halfway]
    back_part = tensor[..., halfway:]
    return jnp.concatenate(
        [
            front_part * cosine - back_part * sine_values,
            back_part * cosine + front_part * sine_values,
        ],
        axis=-1,
    )


def normalize(matrix, gain):
    widened = matrix.astype(jnp.float32)
    return widened * lax.rsqrt(jnp.mean(widened * widened, axis=-1, keepdims=True) + EPSILON) * gain


def request_layout(stretch_owner, counts_row, selected, stretch_len, new_rows):
    slot_total = stretch_owner.shape[0]
    requests = counts_row.shape[0]
    request_ids = jnp.arange(requests, dtype=jnp.int32)
    slot_ids = jnp.arange(slot_total, dtype=jnp.int32)
    belongs = (stretch_owner[:, None] == request_ids[None, :]).astype(jnp.int32)
    first_slot = jnp.sum((stretch_owner[None, :] < request_ids[:, None]).astype(jnp.int32), axis=1)
    stretch_count = jnp.sum(belongs, axis=0)
    offsets = (slot_ids - jnp.sum(belongs * first_slot[None, :], axis=1)) * stretch_len
    inner_ids = jnp.arange(stretch_len, dtype=jnp.int32)
    cache_pos = (offsets[:, None] + inner_ids[None, :]).reshape(-1)
    cache_req = jnp.broadcast_to(stretch_owner[:, None], (slot_total, stretch_len)).reshape(-1)
    cache_ids = jnp.arange(slot_total * stretch_len, dtype=jnp.int32)
    chosen = jnp.sum((selected[:, None] == cache_ids[None, :]).astype(jnp.int32), axis=0)
    cache_live = chosen == 0
    home_slot = ((selected // stretch_len)[:, None] == slot_ids[None, :]).astype(jnp.int32)
    select_req = jnp.sum(home_slot * stretch_owner[None, :], axis=1)
    select_pos = jnp.sum(home_slot * offsets[None, :], axis=1) + selected % stretch_len
    query_total = new_rows - selected.shape[0]
    query_ids = jnp.arange(query_total, dtype=jnp.int32)
    query_start = jnp.cumsum(counts_row) - counts_row
    query_req = jnp.sum((query_ids[:, None] >= query_start[None, 1:]).astype(jnp.int32), axis=1)
    mapping = (query_req[:, None] == request_ids[None, :]).astype(jnp.int32)
    query_pos = (
        jnp.sum(mapping * (stretch_count * stretch_len - query_start)[None, :], axis=1) + query_ids
    )
    row_req = jnp.concatenate([select_req, query_req])
    row_pos = jnp.concatenate([select_pos, query_pos])
    key_req = jnp.concatenate([cache_req, row_req])
    key_pos = jnp.concatenate([cache_pos, row_pos])
    key_live = jnp.concatenate([cache_live, jnp.ones((new_rows,), dtype=bool)])
    return (offsets, row_req, row_pos, key_req, key_pos, key_live)


def attend(queries, all_keys, all_values, row_req, row_pos, key_req, key_pos, key_live):
    scores = jnp.einsum("qcgd,kcd->cgqk", queries, all_keys, preferred_element_type=jnp.float32)
    capped = CAP_VALUE * jnp.tanh(scores * (QUERY_SCALE / CAP_VALUE))
    visible = (
        (key_req[None, :] == row_req[:, None])
        & (key_pos[None, :] <= row_pos[:, None])
        & key_live[None, :]
    ).astype(jnp.float32)
    weights = jnp.exp(capped) * visible[None, None]
    denominator = jnp.sum(weights, axis=-1)
    rounded = weights.astype(jnp.bfloat16)
    weighted = jnp.einsum("cgqk,kcd->qcgd", rounded, all_values, preferred_element_type=jnp.float32)
    result = weighted / jnp.transpose(denominator, (2, 0, 1))[..., None]
    return result.astype(jnp.bfloat16).reshape(queries.shape[0], -1)


def run_attention(query_rot, all_keys, all_values, rows_req, rows_pos, key_req, key_pos, key_live):
    total_rows = query_rot.shape[0]
    block_rows = min(512, total_rows)
    block_total = total_rows // block_rows

    def one_block(bundle):
        return attend(
            bundle[0], all_keys, all_values, bundle[1], bundle[2], key_req, key_pos, key_live
        )

    shaped = query_rot.reshape((block_total, block_rows) + query_rot.shape[1:])
    attended = lax.map(
        one_block,
        (
            shaped,
            rows_req.reshape(block_total, block_rows),
            rows_pos.reshape(block_total, block_rows),
        ),
    )
    return attended.reshape(total_rows, -1)


def on_device(
    hidden,
    input_gain,
    w_query,
    w_key,
    w_value,
    w_out,
    post_gain,
    cache_keys,
    cache_values,
    page_table,
    stretch_request,
    recompute_ids,
    query_counts,
):
    own_rows = hidden[0]
    row_count = own_rows.shape[0]
    tok_total = lax.axis_size("tok")
    new_rows = row_count * tok_total
    stretch_len = cache_keys.shape[1]
    key_heads = w_key.shape[1] // HEAD
    query_heads = w_query.shape[1] // HEAD
    group_size = query_heads // key_heads
    query_cols = w_query.shape[1]
    key_cols = w_key.shape[1]
    normed_own = normalize(own_rows, input_gain).astype(jnp.bfloat16)
    offsets, row_req, row_pos, key_req, key_pos, key_live = request_layout(
        stretch_request[0], query_counts[0], recompute_ids[0], stretch_len, new_rows
    )
    group_index = lax.axis_index("grp")
    my_pages = lax.dynamic_index_in_dim(page_table, group_index, 0, keepdims=False)
    sections = (
        lax.all_gather(cache_keys, "grp", axis=0, tiled=True),
        lax.all_gather(cache_values, "grp", axis=0, tiled=True),
    )
    section_rows = sections[0].shape[0]
    hits = (my_pages[:, None] == jnp.arange(section_rows, dtype=jnp.int32)[None, :]).astype(
        jnp.bfloat16
    )
    picked_keys = jnp.einsum("cp,pkh->ckh", hits, sections[0], preferred_element_type=jnp.float32)
    picked_values = jnp.einsum("cp,pkh->ckh", hits, sections[1], preferred_element_type=jnp.float32)
    page_keys = picked_keys.astype(jnp.bfloat16)
    page_values = picked_values.astype(jnp.bfloat16)
    slot_total = page_keys.shape[0]
    shifts = jnp.broadcast_to(offsets[:, None], (slot_total, stretch_len)).reshape(-1)
    segment = lax.all_gather(normed_own, "tok", axis=0, tiled=True)
    joined = jnp.concatenate(
        [
            jnp.dot(segment, w_query, preferred_element_type=jnp.float32),
            jnp.dot(segment, w_key, preferred_element_type=jnp.float32),
            jnp.dot(segment, w_value, preferred_element_type=jnp.float32),
        ],
        axis=1,
    )
    cached_k = rotate(
        page_keys.astype(jnp.float32).reshape(slot_total * stretch_len, key_heads, HEAD), shifts
    ).astype(jnp.bfloat16)
    cached_v = page_values.reshape(slot_total * stretch_len, key_heads, HEAD)
    query_rot = rotate(joined[:, :query_cols].reshape(new_rows, query_heads, HEAD), row_pos).astype(
        jnp.bfloat16
    )
    query_rot = query_rot.reshape(new_rows, key_heads, group_size, HEAD)
    key_rot = rotate(
        joined[:, query_cols : query_cols + key_cols].reshape(new_rows, key_heads, HEAD), row_pos
    ).astype(jnp.bfloat16)
    value_new = (
        joined[:, query_cols + key_cols :].astype(jnp.bfloat16).reshape(new_rows, key_heads, HEAD)
    )
    all_keys = jnp.concatenate([cached_k, key_rot], axis=0)
    all_values = jnp.concatenate([cached_v, value_new], axis=0)
    attended = run_attention(
        query_rot, all_keys, all_values, row_req, row_pos, key_req, key_pos, key_live
    )
    summed = lax.psum_scatter(
        jnp.dot(attended, w_out, preferred_element_type=jnp.float32).astype(jnp.bfloat16),
        "tok",
        scatter_dimension=0,
        tiled=True,
    ).astype(jnp.float32)
    result = own_rows.astype(jnp.float32) + normalize(summed, post_gain)
    return result.astype(jnp.bfloat16)[None]


def solution(mesh):
    return jax.shard_map(
        on_device,
        mesh=mesh,
        in_specs=(
            P("grp", "tok", None),
            P(),
            P(None, "tok"),
            P(None, "tok"),
            P(None, "tok"),
            P("tok", None),
            P(),
            P("grp", None, "tok"),
            P("grp", None, "tok"),
            P(),
            P("grp", None),
            P("grp", None),
            P("grp", None),
        ),
        out_specs=P("grp", "tok", None),
        check_vma=False,
    )
```

profile of v0, /device:TPU:1, one launch (start us, length us, event | category | flops | bytes accessed | tf_op | source)
XLA Modules:
  0.0 586.5 jit_solution(13476773845455432164)
XLA Ops:
  6.5 2.4 copy.28
  9.0 2.2 copy.32
  11.7 2.1 fusion.30
  16.3 2.8 multiply_cosine_fusion.2
  19.1 51.7 %all-gather.6.cloned.1.call-done = bf16[64,256,128]{2,0,1:T(8,128)(2,1)} async-done(((bf16[8,256,128]{2,0,1:T(8,128)(2,1)}), bf16[64,256,128]{2,0,1:T(8,128)(2,1)}) %all-gather.6.cloned.1.call-update) | async-done | bytes 4194320 | tf_op jit(solution)/shard_map/all_gather | solution.py:141
  70.8 2.9 fusion.33
  75.3 2.3 copy.40
  78.7 54.7 %all-gather.8.cloned.1.call-done = bf16[64,256,128]{2,0,1:T(8,128)(2,1)} async-done(((bf16[8,256,128]{2,0,1:T(8,128)(2,1)}), bf16[64,256,128]{2,0,1:T(8,128)(2,1)}) %all-gather.8.cloned.1.call-update) | async-done | bytes 4194320 | tf_op jit(solution)/shard_map/all_gather | solution.py:142
  133.5 2.9 convolution_convert_fusion.2
  137.2 121.5 %all-gather.4.cloned.1.call-done = bf16[2048,4608]{1,0:T(8,128)(2,1)} async-done(((bf16[128,4608]{1,0:T(8,128)(2,1)}), bf16[2048,4608]{1,0:T(8,128)(2,1)}) %all-gather.4.cloned.1.call-update) | async-done | bytes 18874384 | tf_op jit(solution)/shard_map/all_gather | solution.py:154
  258.7 10.4 %convolution_bitcast_fusion = f32[2048,1,128]{0,2,1:T(8,128)S(1)} fusion(bf16[2048,4608]{1,0:T(8,128)(2,1)} %all-gather.4.cloned.1.call-done, bf16[4608,128]{1,0:T(8,128)(2,1)} %param.18), kind=kOutput, calls=%fused_computation.26 | convolution fusion | flops 2415919104 | bytes 21102592 | tf_op jit(solution)/shard_map/dot_general | solution.py:158
  269.2 5.2 fusion.48
  277.1 9.8 %fusion.63 = f32[2048,256]{0,1:T(8,128)S(1)} fusion(bf16[2048,4608]{1,0:T(8,128)(2,1)} %all-gather.4.cloned.1.call-done, bf16[4608,256]{1,0:T(8,128)(2,1)} %param.17), kind=kOutput, calls=%fused_computation.111 | convolution fusion | flops 4831838208 | bytes 23330816 | tf_op jit(solution)/shard_map/dot_general | solution.py:157
  288.2 2.2 concatenate.67
  290.4 2.2 concatenate.68
  292.7 2.8 pad_maximum_fusion
  295.5 2.6 copy.34
  298.2 9.4 %fusion.32 = bf16[2048,1,128]{2,0,1:T(8,128)(2,1)S(1)} fusion(bf16[2048,4608]{1,0:T(8,128)(2,1)} %all-gather.4.cloned.1.call-done, bf16[4608,128]{1,0:T(8,128)(2,1)} %param.19), kind=kOutput, calls=%fused_computation.34 | convolution fusion | flops 2416181248 | bytes 20578304 | tf_op jit(solution)/shard_map/dot_general | solution.py:159
  308.6 2.3 copy.36
  310.9 98.5 %while.10 = (s32[]{:T(128)}, bf16[4,512,256]{2,1,0:T(8,128)(2,1)}, bf16[4,512,1,2,128]{4,1,3,2,0:T(8,128)(2,1)}, bf16[4096,1,128]{2,0,1:T(8,128)(2,1)S(1)}, s32[...) while((s32[]{:T(128)}, bf16[4,512,256]{2,1,0:T(8,128)(2,1)}, ...), condition=%wide.region_12.13_spmd, body=%wide.region_10.12_spmd.sunk | while | flops 2191784960 | bytes 66643084 | solution.py:98
  310.9 1.8 and_convert_fusion.2
  312.7 9.9 %fusion.80 = (f32[2,512]{1,0:T(2,128)S(1)}, f32[512,2,4096]{2,0,1:T(8,128)}) fusion(f32[512,4096]{1,0:T(8,128)S(1)} %and_convert_fusion.2, bf16[4096,1,128]{2,0,1:T(8,128)(2,1)S(1)} %get-tuple-element.226, bf16[4,512,1,2,128]{4,1,3,2,0:T(8,128)(2,1)} %get-tuple-element.225, s32[]{:T(128)} %get-tuple-element.212), kind=kOutput, calls=%fused_computation.1.clone.1 | convolution fusion | flops 1090518016 | bytes 26481152 | tf_op jit(solution)/shard_map/while/body/eval_jaxpr/qcgd,kcd->cgqk/dot_general | solution.py:72
  322.6 9.4 %fusion.81 = bf16[512,1,2,128]{0,3,2,1:T(8,128)(2,1)} fusion(bf16[4096,1,128]{0,2,1:T(8,128)(2,1)S(1)} %copy-done.1, f32[512,2,4096]{2,0,1:T(8,128)} %get-tuple-element.199, f32[512,4096]{1,0:T(8,128)S(1)} %and_convert_fusion.2, f32[512,2]{0,1:T(2,128)S(1)} %bitcast.153), kind=kOutput, calls=%fused_computation.11.clone.1 | convolution fusion | flops 1090781184 | bytes 26480640 | tf_op jit(solution)/shard_map/while/body/eval_jaxpr/cgqk,kcd->qcgd/dot_general | solution.py:82
  337.4 9.9 %fusion.80 = (f32[2,512]{1,0:T(2,128)S(1)}, f32[512,2,4096]{2,0,1:T(8,128)}) fusion(f32[512,4096]{1,0:T(8,128)S(1)} %and_convert_fusion.2, bf16[4096,1,128]{2,0,1:T(8,128)(2,1)S(1)} %get-tuple-element.226, bf16[4,512,1,2,128]{4,1,3,2,0:T(8,128)(2,1)} %get-tuple-element.225, s32[]{:T(128)} %get-tuple-element.212), kind=kOutput, calls=%fused_computation.1.clone.1 | convolution fusion | flops 1090518016 | bytes 26481152 | tf_op jit(solution)/shard_map/while/body/eval_jaxpr/qcgd,kcd->cgqk/dot_general | solution.py:72
  347.3 9.4 %fusion.81 = bf16[512,1,2,128]{0,3,2,1:T(8,128)(2,1)} fusion(bf16[4096,1,128]{0,2,1:T(8,128)(2,1)S(1)} %copy-done.1, f32[512,2,4096]{2,0,1:T(8,128)} %get-tuple-element.199, f32[512,4096]{1,0:T(8,128)S(1)} %and_convert_fusion.2, f32[512,2]{0,1:T(2,128)S(1)} %bitcast.153), kind=kOutput, calls=%fused_computation.11.clone.1 | convolution fusion | flops 1090781184 | bytes 26480640 | tf_op jit(solution)/shard_map/while/body/eval_jaxpr/cgqk,kcd->qcgd/dot_general | solution.py:82
  362.0 9.9 %fusion.80 = (f32[2,512]{1,0:T(2,128)S(1)}, f32[512,2,4096]{2,0,1:T(8,128)}) fusion(f32[512,4096]{1,0:T(8,128)S(1)} %and_convert_fusion.2, bf16[4096,1,128]{2,0,1:T(8,128)(2,1)S(1)} %get-tuple-element.226, bf16[4,512,1,2,128]{4,1,3,2,0:T(8,128)(2,1)} %get-tuple-element.225, s32[]{:T(128)} %get-tuple-element.212), kind=kOutput, calls=%fused_computation.1.clone.1 | convolution fusion | flops 1090518016 | bytes 26481152 | tf_op jit(solution)/shard_map/while/body/eval_jaxpr/qcgd,kcd->cgqk/dot_general | solution.py:72
  371.9 9.4 %fusion.81 = bf16[512,1,2,128]{0,3,2,1:T(8,128)(2,1)} fusion(bf16[4096,1,128]{0,2,1:T(8,128)(2,1)S(1)} %copy-done.1, f32[512,2,4096]{2,0,1:T(8,128)} %get-tuple-element.199, f32[512,4096]{1,0:T(8,128)S(1)} %and_convert_fusion.2, f32[512,2]{0,1:T(2,128)S(1)} %bitcast.153), kind=kOutput, calls=%fused_computation.11.clone.1 | convolution fusion | flops 1090781184 | bytes 26480640 | tf_op jit(solution)/shard_map/while/body/eval_jaxpr/cgqk,kcd->qcgd/dot_general | solution.py:82
  386.6 9.9 %fusion.80 = (f32[2,512]{1,0:T(2,128)S(1)}, f32[512,2,4096]{2,0,1:T(8,128)}) fusion(f32[512,4096]{1,0:T(8,128)S(1)} %and_convert_fusion.2, bf16[4096,1,128]{2,0,1:T(8,128)(2,1)S(1)} %get-tuple-element.226, bf16[4,512,1,2,128]{4,1,3,2,0:T(8,128)(2,1)} %get-tuple-element.225, s32[]{:T(128)} %get-tuple-element.212), kind=kOutput, calls=%fused_computation.1.clone.1 | convolution fusion | flops 1090518016 | bytes 26481152 | tf_op jit(solution)/shard_map/while/body/eval_jaxpr/qcgd,kcd->cgqk/dot_general | solution.py:72
  396.5 9.4 %fusion.81 = bf16[512,1,2,128]{0,3,2,1:T(8,128)(2,1)} fusion(bf16[4096,1,128]{0,2,1:T(8,128)(2,1)S(1)} %copy-done.1, f32[512,2,4096]{2,0,1:T(8,128)} %get-tuple-element.199, f32[512,4096]{1,0:T(8,128)S(1)} %and_convert_fusion.2, f32[512,2]{0,1:T(2,128)S(1)} %bitcast.153), kind=kOutput, calls=%fused_computation.11.clone.1 | convolution fusion | flops 1090781184 | bytes 26480640 | tf_op jit(solution)/shard_map/while/body/eval_jaxpr/cgqk,kcd->qcgd/dot_general | solution.py:82
  409.4 10.3 %convolution_convert_fusion = bf16[2048,4608]{1,0:T(8,128)(2,1)} fusion(bf16[2048,256]{1,0:T(8,128)(2,1)} %bitcast.152, bf16[256,4608]{1,0:T(8,128)(2,1)S(1)} %copy-done), kind=kOutput, calls=%fused_computation.20 | convolution fusion | flops 4841275392 | bytes 22282240 | tf_op jit(solution)/shard_map/dot_general | solution.py:183
  419.7 156.0 %reduce-scatter.2.cloned.1.call-done = bf16[128,4608]{1,0:T(8,128)(2,1)} async-done(((bf16[2048,4608]{1,0:T(8,128)(2,1)}), bf16[128,4608]{1,0:T(8,128)(2,1)}) %reduce-scatter.2.cloned.1.call-update) | async-done | bytes 1179664 | tf_op jit(solution)/shard_map/reduce_scatter | solution.py:182
  577.2 2.8 fusion.34
  (92 shorter events, 32.6 us)
Async XLA Ops:
  6.5 402.8 %copy-start = (bf16[256,4608]{1,0:T(8,128)(2,1)S(1)}, bf16[256,4608]{1,0:T(8,128)(2,1)}, u32[]{:S(2)}) copy-start(bf16[256,4608]{1,0:T(8,128)(2,1)} %param.20) | copy-start | bytes 7077892
  6.5 4.8 copy-start.2
  6.5 64.3 %all-gather.6.cloned.1.call-start = ((), (), s32[]{:S(2)}) async-start(), calls=%async_computation.2 | async-start | bytes 4718592 | tf_op jit(solution)/shard_map/all_gather | solution.py:141
  9.0 124.5 %all-gather.8.cloned.1.call-start = ((), (), s32[]{:S(2)}) async-start(), calls=%async_computation.3 | async-start | bytes 4718592 | tf_op jit(solution)/shard_map/all_gather | solution.py:142
  11.2 2.6 copy-start.9
  11.2 2.9 copy-start.8
  11.3 3.5 copy-start.7
  11.3 247.5 %all-gather.4.cloned.1.call-start = ((), (), s32[]{:S(2)}) async-start(), calls=%async_computation.1 | async-start | bytes 20054016 | tf_op jit(solution)/shard_map/all_gather | solution.py:154
  13.8 561.9 %reduce-scatter.2.cloned.1.call-start = ((), (), s32[]{:S(2)}) async-start(), calls=%async_computation.4 | async-start | bytes 20054016 | tf_op jit(solution)/shard_map/reduce_scatter | solution.py:182
  277.1 9.8 %copy-start.5 = (f32[2048,64]{0,1:T(8,128)S(1)}, f32[2048,64]{0,1:T(8,128)}, u32[]{:S(2)}) copy-start(f32[2048,64]{0,1:T(8,128)} %get-tuple-element.126) | copy-start | bytes 1572868
  277.1 9.8 %copy-start.6 = (f32[2048,64]{0,1:T(8,128)S(1)}, f32[2048,64]{0,1:T(8,128)}, u32[]{:S(2)}) copy-start(f32[2048,64]{0,1:T(8,128)} %get-tuple-element.127) | copy-start | bytes 1572868
  298.2 9.4 %copy-start.4 = (bf16[8,256,128]{2,1,0:T(8,128)(2,1)S(1)}, bf16[8,256,128]{2,1,0:T(8,128)(2,1)}, u32[]{:S(2)}) copy-start(bf16[8,256,128]{2,1,0:T(8,128)(2,1)} %copy.33) | copy-start | bytes 1572868
  312.7 9.9 %copy-start.1 = (bf16[4096,1,128]{0,2,1:T(8,128)(2,1)S(1)}, bf16[4096,1,128]{0,2,1:T(8,128)(2,1)}, u32[]{:S(2)}) copy-start(bf16[4096,1,128]{0,2,1:T(8,128)(2,1)} %get-tuple-element.232) | copy-start | bytes 3145732 | tf_op jit(solution)/shard_map/while
  337.3 9.9 %copy-start.1 = (bf16[4096,1,128]{0,2,1:T(8,128)(2,1)S(1)}, bf16[4096,1,128]{0,2,1:T(8,128)(2,1)}, u32[]{:S(2)}) copy-start(bf16[4096,1,128]{0,2,1:T(8,128)(2,1)} %get-tuple-element.232) | copy-start | bytes 3145732 | tf_op jit(solution)/shard_map/while
  362.0 9.9 %copy-start.1 = (bf16[4096,1,128]{0,2,1:T(8,128)(2,1)S(1)}, bf16[4096,1,128]{0,2,1:T(8,128)(2,1)}, u32[]{:S(2)}) copy-start(bf16[4096,1,128]{0,2,1:T(8,128)(2,1)} %get-tuple-element.232) | copy-start | bytes 3145732 | tf_op jit(solution)/shard_map/while
  386.6 9.9 %copy-start.1 = (bf16[4096,1,128]{0,2,1:T(8,128)(2,1)S(1)}, bf16[4096,1,128]{0,2,1:T(8,128)(2,1)}, u32[]{:S(2)}) copy-start(bf16[4096,1,128]{0,2,1:T(8,128)(2,1)} %get-tuple-element.232) | copy-start | bytes 3145732 | tf_op jit(solution)/shard_map/while
  419.6 157.6 %copy-start.3 = (bf16[1,128,4608]{2,1,0:T(8,128)(2,1)S(1)}, bf16[1,128,4608]{2,1,0:T(8,128)(2,1)}, u32[]{:S(2)}) copy-start(bf16[1,128,4608]{2,1,0:T(8,128)(2,1)} %param.15) | copy-start | bytes 3538948
Sparse Core Ops, SparseCore 0:
  9.1 61.7 all-gather.5
  72.4 61.0 all-gather.7
  135.9 122.8 all-gather.3
  419.8 155.7 reduce-scatter.1
where the time goes:
time: 588 us; the launch traced here: 587 us
  waiting for transfers between devices  384 us (65%)
  matrix products  123 us (21%)
  local copies, waits for them, and re-layouts  36.6 us (6%)
  other arithmetic  29.6 us (5%)
  between operations  13.4 us (2%)
    reduce_scatter x1, waiting for transfers between devices, on_device(): lax.psum_scatter(jnp.dot(attended, w_out, preferred_element_type=jnp.floa...  156 us
    all_gather x1, waiting for transfers between devices, on_device(): segment = lax.all_gather(normed_own, 'tok', axis=0, tiled=True)  122 us
    all_gather x1, waiting for transfers between devices, on_device(): lax.all_gather(cache_values, 'grp', axis=0, tiled=True)  54.7 us
    all_gather x1, waiting for transfers between devices, on_device(): lax.all_gather(cache_keys, 'grp', axis=0, tiled=True)  51.7 us
    dot_general x4, matrix products, attend(): jnp.einsum('qcgd,kcd->cgqk', queries, all_keys, preferred_element_type=jn...  39.7 us
    dot_general x4, matrix products, attend(): jnp.einsum('cgqk,kcd->qcgd', rounded, all_values, preferred_element_type=...  37.4 us
    dynamic_update_slice x8, local copies, waits for them, and re-layouts, run_attention(): lax.map(one_block, (shaped, rows_req.reshape(block_total, block_rows), ro...  13.9 us
  transfers between devices with their start and end apart: 4, of which 4 were waited for; matrix products, arithmetic and copies ran while one was open for 4% of the time, Pallas kernels for 0%

commit v1 on v0

--- a/solution.py
+++ b/solution.py
@@ -151,7 +151,8 @@
     page_values = picked_values.astype(jnp.bfloat16)
     slot_total = page_keys.shape[0]
     shifts = jnp.broadcast_to(offsets[:, None], (slot_total, stretch_len)).reshape(-1)
-    segment = lax.all_gather(normed_own, "tok", axis=0, tiled=True)
+    sent = jnp.stack([normed_own] * lax.axis_size("tok"))
+    segment = jnp.concatenate(lax.all_to_all(sent, "tok", 0, 0), axis=0)
     joined = jnp.concatenate(
         [
             jnp.dot(segment, w_query, preferred_element_type=jnp.float32),

time: 588 us -> 669 us (1.14)
  waiting for transfers between devices: 384 us -> 449 us
  starting transfers between devices: 0.13 us -> 8.7 us
    all_gather x1, waiting for transfers between devices: 51.7 us -> 227 us  [on_device(): lax.all_gather(cache_keys, 'grp', axis=0, tiled=True)]
    all_gather x1 -> x0, waiting for transfers between devices: 122 us -> none  [on_device(): segment = lax.all_gather(normed_own, 'tok', axis=0, tiled=True)]
    all_to_all x0 -> x1, starting transfers between devices: none -> 8.58 us  [on_device(): segment = jnp.concatenate(lax.all_to_all(sent, 'tok', 0, 0), axis=0)]
    another operation x0 -> x1, local copies, waits for them, and re-layouts: none -> 6.82 us  [on_device(): sent = jnp.stack([normed_own] * lax.axis_size('tok'))]
  transfers between devices with their start and end apart: 4 -> 4, of which waited for: 4 -> 3; matrix products, arithmetic and copies ran while one was open for 4% -> 4% of each run, Pallas kernels for 0% -> 0%
where the time goes in v1:
time: 669 us; the launch traced here: 668 us
  waiting for transfers between devices  449 us (67%)
  matrix products  123 us (18%)
  local copies, waits for them, and re-layouts  42.9 us (6%)
  other arithmetic  30.7 us (5%)
  between operations  13.4 us (2%)
  starting transfers between devices  8.7 us (1%)
    all_gather x1, waiting for transfers between devices, on_device(): lax.all_gather(cache_keys, 'grp', axis=0, tiled=True)  227 us
    reduce_scatter x1, waiting for transfers between devices, on_device(): lax.psum_scatter(jnp.dot(attended, w_out, preferred_element_type=jnp.floa...  161 us
    all_gather x1, waiting for transfers between devices, on_device(): lax.all_gather(cache_values, 'grp', axis=0, tiled=True)  60.2 us
    dot_general x4, matrix products, attend(): jnp.einsum('qcgd,kcd->cgqk', queries, all_keys, preferred_element_type=jn...  39.6 us
    dot_general x4, matrix products, attend(): jnp.einsum('cgqk,kcd->qcgd', rounded, all_values, preferred_element_type=...  37.5 us
    dynamic_update_slice x8, local copies, waits for them, and re-layouts, run_attention(): lax.map(one_block, (shaped, rows_req.reshape(block_total, block_rows), ro...  13.8 us
  transfers between devices with their start and end apart: 4, of which 3 were waited for; matrix products, arithmetic and copies ran while one was open for 4% of the time, Pallas kernels for 0%

profile of v1, /device:TPU:1, one launch (start us, length us, event | category | flops | bytes accessed | tf_op | source)
XLA Modules:
  0.0 667.6 jit_solution(11832511244407896080)
XLA Ops:
  9.9 6.8 %stack.5 = bf16[16,128,4608]{2,1,0:T(8,128)(2,1)} broadcast(bf16[128,4608]{1,0:T(8,128)(2,1)S(1)} %fusion.36), dimensions={1,2} | broadcast | bytes 20054016 | tf_op jit(solution)/shard_map/stack | solution.py:154
  16.7 8.6 %all-to-all-start = ((bf16[16,128,4608]{2,1,0:T(8,128)(2,1)}), bf16[16,128,4608]{2,1,0:T(8,128)(2,1)}, u32[]{:S(2)}, u32[]{:S(2)}) async-start(bf16[16,128,4608]{2,1,0:T(8,128)(2,1)} %stack.5), calls=%async_computation | async-start | bytes 37748736 | tf_op jit(solution)/shard_map/all_to_all | solution.py:155
  27.9 4.3 copy.45
  34.7 2.8 multiply_cosine_fusion.2
  37.5 227.3 %all-gather.3.cloned.1.call-done = bf16[64,256,128]{2,0,1:T(8,128)(2,1)} async-done(((bf16[8,256,128]{2,0,1:T(8,128)(2,1)}), bf16[64,256,128]{2,0,1:T(8,128)(2,1)}) %all-gather.3.cloned.1.call-update) | async-done | bytes 4194320 | tf_op jit(solution)/shard_map/all_gather | solution.py:141
  264.7 2.9 fusion.35
  269.2 2.3 copy.49
  272.7 60.2 %all-gather.5.cloned.1.call-done = bf16[64,256,128]{2,0,1:T(8,128)(2,1)} async-done(((bf16[8,256,128]{2,0,1:T(8,128)(2,1)}), bf16[64,256,128]{2,0,1:T(8,128)(2,1)}) %all-gather.5.cloned.1.call-update) | async-done | bytes 4194320 | tf_op jit(solution)/shard_map/all_gather | solution.py:142
  332.9 2.9 convolution_convert_fusion.2
  336.7 9.8 %fusion.66 = f32[2048,2,128]{0,2,1:T(8,128)S(1)} fusion(bf16[2048,4608,1]{1,0,2:T(8,128)(2,1)} %bitcast.21, bf16[2,128,4608]{2,1,0:T(8,128)(2,1)} %bitcast.164), kind=kOutput, calls=%fused_computation.113 | convolution fusion | flops 4831838208 | bytes 23330816 | tf_op jit(solution)/shard_map/dot_general | solution.py:158
  352.3 10.4 %convolution_bitcast_fusion = f32[2048,1,128]{0,2,1:T(8,128)S(1)} fusion(bf16[2048,4608]{1,0:T(8,128)(2,1)} %bitcast.20, bf16[4608,128]{1,0:T(8,128)(2,1)} %param.18), kind=kOutput, calls=%fused_computation.27 | convolution fusion | flops 2415919104 | bytes 21102592 | tf_op jit(solution)/shard_map/dot_general | solution.py:159
  362.7 5.2 fusion.51
  370.6 9.4 %fusion.34 = bf16[2048,1,128]{2,0,1:T(8,128)(2,1)S(1)} fusion(bf16[2048,4608]{1,0:T(8,128)(2,1)} %bitcast.20, bf16[4608,128]{1,0:T(8,128)(2,1)} %param.19), kind=kOutput, calls=%fused_computation.35 | convolution fusion | flops 2416181248 | bytes 20578304 | tf_op jit(solution)/shard_map/dot_general | solution.py:160
  381.1 2.3 copy.43
  383.4 3.2 pad_maximum_fusion
  386.5 98.4 %while.10 = (s32[]{:T(128)}, bf16[4,512,256]{2,1,0:T(8,128)(2,1)}, bf16[4,512,1,2,128]{4,1,3,2,0:T(8,128)(2,1)}, bf16[4096,1,128]{2,0,1:T(8,128)(2,1)S(1)}, s32[...) while((s32[]{:T(128)}, bf16[4,512,256]{2,1,0:T(8,128)(2,1)}, ...), condition=%wide.region_12.13_spmd, body=%wide.region_10.12_spmd.sunk | while | flops 2191784960 | bytes 66642076 | solution.py:98
  386.5 1.8 and_convert_fusion.2
  388.4 9.9 %fusion.83 = (f32[2,512]{1,0:T(2,128)S(1)}, f32[512,2,4096]{2,0,1:T(8,128)}) fusion(f32[512,4096]{1,0:T(8,128)S(1)} %and_convert_fusion.2, bf16[4096,1,128]{2,0,1:T(8,128)(2,1)S(1)} %get-tuple-element.226, bf16[4,512,1,2,128]{4,1,3,2,0:T(8,128)(2,1)} %get-tuple-element.225, s32[]{:T(128)S(6)} %copy.58), kind=kOutput, calls=%fused_computation.1.clone.1 | convolution fusion | flops 1090518016 | bytes 26480644 | tf_op jit(solution)/shard_map/while/body/eval_jaxpr/qcgd,kcd->cgqk/dot_general | solution.py:72
  398.3 9.4 %fusion.84 = bf16[512,1,2,128]{0,3,2,1:T(8,128)(2,1)} fusion(bf16[4096,1,128]{0,2,1:T(8,128)(2,1)S(1)} %copy-done.1, f32[512,2,4096]{2,0,1:T(8,128)} %get-tuple-element.199, f32[512,4096]{1,0:T(8,128)S(1)} %and_convert_fusion.2, f32[512,2]{0,1:T(2,128)S(1)} %bitcast.167), kind=kOutput, calls=%fused_computation.11.clone.1 | convolution fusion | flops 1090781184 | bytes 26480640 | tf_op jit(solution)/shard_map/while/body/eval_jaxpr/cgqk,kcd->qcgd/dot_general | solution.py:82
  411.1 1.8 and_convert_fusion.2
  413.0 9.9 %fusion.83 = (f32[2,512]{1,0:T(2,128)S(1)}, f32[512,2,4096]{2,0,1:T(8,128)}) fusion(f32[512,4096]{1,0:T(8,128)S(1)} %and_convert_fusion.2, bf16[4096,1,128]{2,0,1:T(8,128)(2,1)S(1)} %get-tuple-element.226, bf16[4,512,1,2,128]{4,1,3,2,0:T(8,128)(2,1)} %get-tuple-element.225, s32[]{:T(128)S(6)} %copy.58), kind=kOutput, calls=%fused_computation.1.clone.1 | convolution fusion | flops 1090518016 | bytes 26480644 | tf_op jit(solution)/shard_map/while/body/eval_jaxpr/qcgd,kcd->cgqk/dot_general | solution.py:72
  422.9 9.4 %fusion.84 = bf16[512,1,2,128]{0,3,2,1:T(8,128)(2,1)} fusion(bf16[4096,1,128]{0,2,1:T(8,128)(2,1)S(1)} %copy-done.1, f32[512,2,4096]{2,0,1:T(8,128)} %get-tuple-element.199, f32[512,4096]{1,0:T(8,128)S(1)} %and_convert_fusion.2, f32[512,2]{0,1:T(2,128)S(1)} %bitcast.167), kind=kOutput, calls=%fused_computation.11.clone.1 | convolution fusion | flops 1090781184 | bytes 26480640 | tf_op jit(solution)/shard_map/while/body/eval_jaxpr/cgqk,kcd->qcgd/dot_general | solution.py:82
  432.3 1.8 copy.54
  435.7 1.8 and_convert_fusion.2
  437.6 9.9 %fusion.83 = (f32[2,512]{1,0:T(2,128)S(1)}, f32[512,2,4096]{2,0,1:T(8,128)}) fusion(f32[512,4096]{1,0:T(8,128)S(1)} %and_convert_fusion.2, bf16[4096,1,128]{2,0,1:T(8,128)(2,1)S(1)} %get-tuple-element.226, bf16[4,512,1,2,128]{4,1,3,2,0:T(8,128)(2,1)} %get-tuple-element.225, s32[]{:T(128)S(6)} %copy.58), kind=kOutput, calls=%fused_computation.1.clone.1 | convolution fusion | flops 1090518016 | bytes 26480644 | tf_op jit(solution)/shard_map/while/body/eval_jaxpr/qcgd,kcd->cgqk/dot_general | solution.py:72
  447.5 9.4 %fusion.84 = bf16[512,1,2,128]{0,3,2,1:T(8,128)(2,1)} fusion(bf16[4096,1,128]{0,2,1:T(8,128)(2,1)S(1)} %copy-done.1, f32[512,2,4096]{2,0,1:T(8,128)} %get-tuple-element.199, f32[512,4096]{1,0:T(8,128)S(1)} %and_convert_fusion.2, f32[512,2]{0,1:T(2,128)S(1)} %bitcast.167), kind=kOutput, calls=%fused_computation.11.clone.1 | convolution fusion | flops 1090781184 | bytes 26480640 | tf_op jit(solution)/shard_map/while/body/eval_jaxpr/cgqk,kcd->qcgd/dot_general | solution.py:82
  460.3 1.8 and_convert_fusion.2
  462.2 9.9 %fusion.83 = (f32[2,512]{1,0:T(2,128)S(1)}, f32[512,2,4096]{2,0,1:T(8,128)}) fusion(f32[512,4096]{1,0:T(8,128)S(1)} %and_convert_fusion.2, bf16[4096,1,128]{2,0,1:T(8,128)(2,1)S(1)} %get-tuple-element.226, bf16[4,512,1,2,128]{4,1,3,2,0:T(8,128)(2,1)} %get-tuple-element.225, s32[]{:T(128)S(6)} %copy.58), kind=kOutput, calls=%fused_computation.1.clone.1 | convolution fusion | flops 1090518016 | bytes 26480644 | tf_op jit(solution)/shard_map/while/body/eval_jaxpr/qcgd,kcd->cgqk/dot_general | solution.py:72
  472.1 9.4 %fusion.84 = bf16[512,1,2,128]{0,3,2,1:T(8,128)(2,1)} fusion(bf16[4096,1,128]{0,2,1:T(8,128)(2,1)S(1)} %copy-done.1, f32[512,2,4096]{2,0,1:T(8,128)} %get-tuple-element.199, f32[512,4096]{1,0:T(8,128)S(1)} %and_convert_fusion.2, f32[512,2]{0,1:T(2,128)S(1)} %bitcast.167), kind=kOutput, calls=%fused_computation.11.clone.1 | convolution fusion | flops 1090781184 | bytes 26480640 | tf_op jit(solution)/shard_map/while/body/eval_jaxpr/cgqk,kcd->qcgd/dot_general | solution.py:82
  484.9 10.3 %convolution_convert_fusion = bf16[2048,4608]{1,0:T(8,128)(2,1)} fusion(bf16[2048,256]{1,0:T(8,128)(2,1)} %bitcast.166, bf16[256,4608]{1,0:T(8,128)(2,1)S(1)} %copy-done), kind=kOutput, calls=%fused_computation.20 | convolution fusion | flops 4841275392 | bytes 22282240 | tf_op jit(solution)/shard_map/dot_general | solution.py:184
  495.2 161.5 %reduce-scatter.2.cloned.1.call-done = bf16[128,4608]{1,0:T(8,128)(2,1)} async-done(((bf16[2048,4608]{1,0:T(8,128)(2,1)}), bf16[128,4608]{1,0:T(8,128)(2,1)}) %reduce-scatter.2.cloned.1.call-update) | async-done | bytes 1179664 | tf_op jit(solution)/shard_map/reduce_scatter | solution.py:183
  658.3 2.8 fusion.37
  (96 shorter events, 35.1 us)
Async XLA Ops:
  6.5 478.4 %copy-start = (bf16[256,4608]{1,0:T(8,128)(2,1)S(1)}, bf16[256,4608]{1,0:T(8,128)(2,1)}, u32[]{:S(2)}) copy-start(bf16[256,4608]{1,0:T(8,128)(2,1)} %param.20) | copy-start | bytes 7077892
  16.7 8.6 %copy-start.6 = (bf16[8,256,128]{2,1,0:T(8,128)(2,1)S(1)}, bf16[8,256,128]{2,1,0:T(8,128)(2,1)}, u32[]{:S(2)}) copy-start(bf16[8,256,128]{2,1,0:T(8,128)(2,1)} %param.22) | copy-start | bytes 1572868
  16.7 9.8 %copy-start.7 = (bf16[8,256,128]{2,1,0:T(8,128)(2,1)S(1)}, bf16[8,256,128]{2,1,0:T(8,128)(2,1)}, u32[]{:S(2)}) copy-start(bf16[8,256,128]{2,1,0:T(8,128)(2,1)} %param.23) | copy-start | bytes 1572868
  16.7 320.0 %all-to-all-start = ((bf16[16,128,4608]{2,1,0:T(8,128)(2,1)}), bf16[16,128,4608]{2,1,0:T(8,128)(2,1)}, u32[]{:S(2)}, u32[]{:S(2)}) async-start(bf16[16,128,4608]{2,1,0:T(8,128)(2,1)} %stack.5), calls=%async_computation | async-start | bytes 37748736 | tf_op jit(solution)/shard_map/all_to_all | solution.py:155
  25.3 239.4 %all-gather.3.cloned.1.call-start = ((), (), s32[]{:S(2)}) async-start(), calls=%async_computation.2 | async-start | bytes 4718592 | tf_op jit(solution)/shard_map/all_gather | solution.py:141
  26.5 306.4 %all-gather.5.cloned.1.call-start = ((), (), s32[]{:S(2)}) async-start(), calls=%async_computation.3 | async-start | bytes 4718592 | tf_op jit(solution)/shard_map/all_gather | solution.py:142
  27.8 628.9 %reduce-scatter.2.cloned.1.call-start = ((), (), s32[]{:S(2)}) async-start(), calls=%async_computation.4 | async-start | bytes 20054016 | tf_op jit(solution)/shard_map/reduce_scatter | solution.py:183
  27.9 4.4 copy-start.10
  27.9 4.6 copy-start.9
  27.9 5.1 copy-start.8
  336.7 9.8 %copy-start.4 = (f32[2048,64]{0,1:T(8,128)S(1)}, f32[2048,64]{0,1:T(8,128)}, u32[]{:S(2)}) copy-start(f32[2048,64]{0,1:T(8,128)} %get-tuple-element.126) | copy-start | bytes 1572868
  336.7 9.8 %copy-start.5 = (f32[2048,64]{0,1:T(8,128)S(1)}, f32[2048,64]{0,1:T(8,128)}, u32[]{:S(2)}) copy-start(f32[2048,64]{0,1:T(8,128)} %get-tuple-element.127) | copy-start | bytes 1572868
  370.6 9.4 %copy-start.3 = (bf16[8,256,128]{2,1,0:T(8,128)(2,1)S(1)}, bf16[8,256,128]{2,1,0:T(8,128)(2,1)}, u32[]{:S(2)}) copy-start(bf16[8,256,128]{2,1,0:T(8,128)(2,1)} %copy.41) | copy-start | bytes 1572868
  388.4 9.9 %copy-start.1 = (bf16[4096,1,128]{0,2,1:T(8,128)(2,1)S(1)}, bf16[4096,1,128]{0,2,1:T(8,128)(2,1)}, u32[]{:S(2)}) copy-start(bf16[4096,1,128]{0,2,1:T(8,128)(2,1)} %get-tuple-element.232) | copy-start | bytes 3145732 | tf_op jit(solution)/shard_map/while
  413.0 9.9 %copy-start.1 = (bf16[4096,1,128]{0,2,1:T(8,128)(2,1)S(1)}, bf16[4096,1,128]{0,2,1:T(8,128)(2,1)}, u32[]{:S(2)}) copy-start(bf16[4096,1,128]{0,2,1:T(8,128)(2,1)} %get-tuple-element.232) | copy-start | bytes 3145732 | tf_op jit(solution)/shard_map/while
  437.6 9.9 %copy-start.1 = (bf16[4096,1,128]{0,2,1:T(8,128)(2,1)S(1)}, bf16[4096,1,128]{0,2,1:T(8,128)(2,1)}, u32[]{:S(2)}) copy-start(bf16[4096,1,128]{0,2,1:T(8,128)(2,1)} %get-tuple-element.232) | copy-start | bytes 3145732 | tf_op jit(solution)/shard_map/while
  462.1 9.9 %copy-start.1 = (bf16[4096,1,128]{0,2,1:T(8,128)(2,1)S(1)}, bf16[4096,1,128]{0,2,1:T(8,128)(2,1)}, u32[]{:S(2)}) copy-start(bf16[4096,1,128]{0,2,1:T(8,128)(2,1)} %get-tuple-element.232) | copy-start | bytes 3145732 | tf_op jit(solution)/shard_map/while
  495.2 163.1 %copy-start.2 = (bf16[1,128,4608]{2,1,0:T(8,128)(2,1)S(1)}, bf16[1,128,4608]{2,1,0:T(8,128)(2,1)}, u32[]{:S(2)}) copy-start(bf16[1,128,4608]{2,1,0:T(8,128)(2,1)} %param.15) | copy-start | bytes 3538948
Sparse Core Ops, SparseCore 0:
  27.7 236.9 all-gather.2
  266.3 66.5 all-gather.4
  495.3 161.3 reduce-scatter.1
